TPU v7x, 32 devices: a whole 2x2x4 slice. The times are simulated.
32 devices in a mesh: groups: 2 (over y), seq: 4 (over z), batch: 2 (over x), sub: 2 (over core).
Axes of the slice: x: 2, y: 2, z: 4, core: 2. Of those that a mesh axis runs over, the one named last changes fastest.
Arguments:
- gen_hidden: bfloat16 [4, 256, 8192], P(('groups', 'batch'), None, ('seq', 'sub')), parts along dimension 0, may hold values from -6 to 6
- out_proj: bfloat16 [8192, 4096], P(('seq', 'sub')), may hold values from -0.0625 to 0.0625
- norm_gain: bfloat16 [4096], replicated, may hold values from 0.099609375 to 1.8984375
- q_weight: bfloat16 [4096, 4096], P(None, ('seq', 'sub')), may hold values from -0.09375 to 0.09375
- kv_weight: bfloat16 [2, 4096, 1024], P(None, None, ('seq', 'sub')), may hold values from -0.09375 to 0.09375
- kv_cache: bfloat16 [2, 4, 8192, 1024], P(None, ('groups', 'batch'), ('seq', 'sub')), parts along dimension 1, may hold values from -96 to 96
- lengths: int32 [4], P(('groups', 'batch')), parts along dimension 0, may hold values from 1024 to 8192, as said below
- span_start: int32 [4], P(('groups', 'batch')), parts along dimension 0, may hold values from 1024 to 16383, as said below
Outputs:
- attention: bfloat16 [4, 256, 4096], P(('groups', 'batch'), ('seq', 'sub')), parts along dimension 0
There are 2 independent parts, one for each index of `groups`. A program takes and returns all parts, laid end to end along the dimension named above; an argument that names none is the same for every part. Nothing has to cross between parts.
Inputs may be any that keep to these rules, and one draw needn't show every extreme that they name: `lengths`: slots at or past a session's length are not attended. In every draw some session has the full 8192 slots. `span_start`: A session's span starts at or after its window length and less than 8192 later.
All inputs are finite; a program needn't handle non-finite values.
Results may differ from a plain program's by a relative error of at most 0.04.
Values may be sent and summed in bfloat16 or wider, within the bound.
A program may use at most 128 MiB of HBM per device.

v0:
```python
import math

import jax
import jax.numpy as jnp
from jax import lax
from jax.sharding import PartitionSpec as P

QH = 32
KVH = 8
HD = 128


EPS = 1e-05
THETA = 500000.0
NEG = -1e30


def rotate(values, positions):
    half = values.shape[-1] // 2
    freq = THETA ** (-jnp.arange(half, dtype=jnp.float32) * 2.0 / values.shape[-1])
    angle = positions.astype(jnp.float32)[..., None] * freq
    cosine = jnp.cos(angle)[..., None, :]
    sine = jnp.sin(angle)[..., None, :]
    first = values[..., :half]
    second = values[..., half:]
    return jnp.concatenate(
        [first * cosine - second * sine, second * cosine + first * sine], axis=-1
    )


def body(gen_hidden, out_proj, norm_gain, q_weight, kv_weight, kv_cache, lengths, span_start):
    sessions, span, _ = gen_hidden.shape
    shards = lax.axis_size(("seq", "sub"))
    mine = lax.axis_index(("seq", "sub"))
    rows = span // shards
    local_heads = q_weight.shape[1] // HD
    group = QH // KVH
    scale = 1.0 / math.sqrt(HD)
    window_local = kv_cache.shape[2]
    summed = lax.psum(
        jnp.einsum("sci,id->csd", gen_hidden, out_proj, preferred_element_type=jnp.float32),
        ("seq", "sub"),
    )
    inputs = summed.astype(jnp.bfloat16)
    wide = inputs.astype(jnp.float32)
    inverse = lax.rsqrt(jnp.mean(wide * wide, axis=-1, keepdims=True) + EPS)
    normed = (wide * inverse * norm_gain.astype(jnp.float32)).astype(jnp.bfloat16)
    positions = span_start[None, :] + jnp.arange(span, dtype=jnp.int32)[:, None]
    query = jnp.einsum("csd,dh->csh", normed, q_weight, preferred_element_type=jnp.float32)
    query = rotate(query.reshape(span, sessions, local_heads, HD), positions).astype(jnp.bfloat16)
    kv_raw = jnp.einsum(
        "csd,jdk->jcsk", normed, kv_weight, preferred_element_type=jnp.float32
    ).astype(jnp.bfloat16)
    query_rows = jnp.arange(span, dtype=jnp.int32)
    new_rows = lax.all_to_all(kv_raw, ("seq", "sub"), split_axis=1, concat_axis=3, tiled=True)
    my_positions = lax.dynamic_slice_in_dim(positions, mine * rows, rows, 0)
    new_keys = rotate(
        new_rows[0].reshape(rows, sessions, KVH, HD).astype(jnp.float32), my_positions
    ).astype(jnp.bfloat16)
    new_values = new_rows[1].reshape(rows, sessions, KVH, HD)
    every_query = lax.all_gather(
        query.reshape(span, sessions, local_heads * HD), ("seq", "sub"), axis=2, tiled=True
    )
    grouped = every_query.reshape(span, sessions, KVH, group, HD)
    cached = kv_cache.reshape(2, sessions, window_local, KVH, HD)
    cache_scores = (
        jnp.einsum("csagh,swah->sagcw", grouped, cached[0], preferred_element_type=jnp.float32)
        * scale
    )
    slots = mine * window_local + jnp.arange(window_local, dtype=jnp.int32)
    live = slots[None, :] < lengths[:, None]
    cache_scores = jnp.where(live[:, None, None, None, :], cache_scores, NEG)
    span_scores = (
        jnp.einsum("csagh,tsah->sagct", grouped, new_keys, preferred_element_type=jnp.float32)
        * scale
    )
    key_rows = mine * rows + jnp.arange(rows, dtype=jnp.int32)
    causal = key_rows[None, :] <= query_rows[:, None]
    span_scores = jnp.where(causal, span_scores, NEG)
    top = jnp.maximum(jnp.max(cache_scores, axis=-1), jnp.max(span_scores, axis=-1))
    cache_weights = jnp.exp(cache_scores - top[..., None])
    span_weights = jnp.exp(span_scores - top[..., None])
    total = jnp.sum(cache_weights, axis=-1) + jnp.sum(span_weights, axis=-1)
    mixed = jnp.einsum(
        "sagcw,swah->scagh",
        cache_weights.astype(jnp.bfloat16),
        cached[1],
        preferred_element_type=jnp.float32,
    )
    mixed = mixed + jnp.einsum(
        "sagct,tsah->scagh",
        span_weights.astype(jnp.bfloat16),
        new_values,
        preferred_element_type=jnp.float32,
    )
    partial_value = mixed.reshape(1, sessions, span, QH * HD)
    peak = jnp.transpose(top, (0, 3, 1, 2)).reshape(1, sessions, span, QH)
    mass = jnp.transpose(total, (0, 3, 1, 2)).reshape(1, sessions, span, QH)
    pieces, peaks, masses = (
        lax.all_to_all(
            partial_value.astype(jnp.bfloat16),
            ("seq", "sub"),
            split_axis=2,
            concat_axis=0,
            tiled=True,
        ).astype(partial_value.dtype),
        lax.all_to_all(
            peak.astype(jnp.bfloat16), ("seq", "sub"), split_axis=2, concat_axis=0, tiled=True
        ).astype(peak.dtype),
        lax.all_to_all(
            mass.astype(jnp.bfloat16), ("seq", "sub"), split_axis=2, concat_axis=0, tiled=True
        ).astype(mass.dtype),
    )
    best = jnp.max(peaks, axis=0)
    factor = jnp.exp(peaks - best[None])
    numer = jnp.sum(factor[..., None] * pieces.reshape(shards, sessions, rows, QH, HD), axis=0)
    denom = jnp.sum(factor * masses, axis=0)
    return (numer / denom[..., None]).astype(jnp.bfloat16).reshape(sessions, rows, QH * HD)


def solution(mesh):
    placed = (
        P(("groups", "batch"), None, ("seq", "sub")),
        P(("seq", "sub"), None),
        P(),
        P(None, ("seq", "sub")),
        P(None, None, ("seq", "sub")),
        P(None, ("groups", "batch"), ("seq", "sub"), None),
        P(("groups", "batch")),
        P(("groups", "batch")),
    )
    return jax.shard_map(
        body,
        mesh=mesh,
        in_specs=placed,
        out_specs=P(("groups", "batch"), ("seq", "sub"), None),
        check_vma=False,
    )
```

profile of v0, /device:TPU:0, one launch (start us, length us, event | category | flops | bytes accessed | tf_op | source)
XLA Modules:
  0.0 313.5 jit_solution(3621349744823222780)
XLA Ops:
  8.1 7.8 %convolution_bitcast_fusion = f32[256,1,4096]{0,2,1:T(8,128)} fusion(bf16[1024,4096]{1,0:T(8,128)(2,1)} %param.9, bf16[1,256,1024]{2,1,0:T(8,128)(2,1)} %param.8), kind=kOutput, calls=%fused_computation.9 | convolution fusion | flops 2147483648 | bytes 13107200 | tf_op jit(solution)/shard_map/sci,id->csd/dot_general | solution.py:41
  15.9 90.9 %all-reduce.1 = bf16[256,1,4096]{0,2,1:T(8,128)(2,1)} all-reduce(f32[256,1,4096]{0,2,1:T(8,128)} %convolution_bitcast_fusion), channel_id=1, replica_groups=mesh['groups'=2,'seq'=4,'batch'=2,'sub'=2] {'seq','sub'}, use_global_device_ids=true, to_apply=%region_0.0 | all-reduce | flops 1048576 | bytes 6291456 | tf_op jit(solution)/shard_map/psum | solution.py:40
  106.8 2.2 fusion.8
  109.0 6.4 %copy.69 = bf16[512,4096]{1,0:T(8,128)(2,1)} copy(bf16[512,4096]{0,1:T(8,128)(2,1)} %bitcast.162) | data formatting | bytes 8388608 | tf_op jit(solution)/shard_map/reshape.177
  115.7 4.2 %convolution_bitcast_fusion.1 = f32[256,1,4,128]{0,3,2,1:T(8,128)S(1)} fusion(bf16[4,128,4096]{2,1,0:T(8,128)(2,1)} %bitcast.163, f32[4096]{0:T(1024)S(1)} %convert_element_type.207, f32[256]{0:T(256)S(1)} %add_rsqrt_fusion, bf16[256,1,4096]{0,2,1:T(8,128)(2,1)} %all-reduce.1), kind=kOutput, calls=%fused_computation.22 | convolution fusion | flops 1077936128 | bytes 6833152 | tf_op jit(solution)/shard_map/csd,dh->csh/dot_general | solution.py:49
  120.8 3.0 fusion.17
  124.5 3.6 %all-to-all-start = ((bf16[2,256,1,128]{3,0,2,1:T(2,128)(2,1)}), bf16[2,256,1,128]{3,0,2,1:T(2,128)(2,1)S(1)}, u32[]{:S(2)}, u32[]{:S(2)}) async-start(bf16[2,256,1,128]{3,0,2,1:T(2,128)(2,1)} %copy.48), calls=%async_computation | async-start | bytes 262144 | tf_op jit(solution)/shard_map/all_to_all | solution.py:55
  128.8 4.0 %fusion.38 = (bf16[1,1,1024,1024]{3,2,1,0:T(8,128)(2,1)S(1)}, bf16[1,1,1024,1024]{3,2,1,0:T(8,128)(2,1)}) fusion(bf16[2,1,1024,1024]{3,2,1,0:T(8,128)(2,1)} %param.13), kind=kLoop, calls=%fused_computation.67 | loop fusion | bytes 8388608 | tf_op jit(solution)/shard_map/slice | solution.py:87
  132.9 2.5 copy.54
  135.4 2.9 copy.73
  138.6 14.2 %all-gather.2.cloned.1.call-done = bf16[256,1,4096]{0,2,1:T(8,128)(2,1)} async-done(((bf16[256,1,512]{0,2,1:T(8,128)(2,1)}), bf16[256,1,4096]{0,2,1:T(8,128)(2,1)}) %all-gather.2.cloned.1.call-update) | async-done | bytes 2097168 | tf_op jit(solution)/shard_map/all_gather | solution.py:61
  152.8 15.6 %fusion.3 = (f32[8,4,256]{2,1,0:T(4,128)S(1)}, f32[8,256,4,1024]{3,1,2,0:T(8,128)}) fusion(pred[1024]{0:T(1024)(128)(4,1)S(1)} %add_compare_fusion, bf16[256,8,4,128]{0,3,2,1:T(8,128)(2,1)} %bitcast.159, bf16[1024,8,128,1]{0,2,3,1:T(8,128)(2,1)S(1)} %bitcast.161), kind=kOutput, calls=%fused_computation.5 | convolution fusion | flops 2172641280 | bytes 37782528 | tf_op jit(solution)/shard_map/csagh,swah->sagcw/dot_general | solution.py:67
  169.0 14.6 %fusion.1 = f32[8,4,256]{2,1,0:T(4,128)S(1)} fusion(f32[8,256,4,1024]{3,1,2,0:T(8,128)} %get-tuple-element.18, f32[8,4,256]{2,1,0:T(4,128)S(1)} %get-tuple-element.6, pred[1024]{0:T(1024)(128)(4,1)S(1)} %add_compare_fusion), kind=kLoop, calls=%fused_computation.3 | loop fusion | flops 33546240 | bytes 33620992 | tf_op jit(solution)/shard_map/reduce_sum | solution.py:83
  186.2 3.3 %all-to-all-start.3 = ((bf16[8,2,512]{2,1,0:T(2,128)(2,1)}), bf16[8,2,512]{2,1,0:T(2,128)(2,1)S(1)}, u32[]{:S(2)}, u32[]{:S(2)}) async-start(bf16[8,2,512]{2,1,0:T(2,128)(2,1)} %reshape.508), calls=%async_computation.3 | async-start | bytes 32768 | tf_op jit(solution)/shard_map/all_to_all | solution.py:110
  189.5 2.8 fusion.21
  195.1 4.0 %all-to-all-start.1 = ((bf16[8,2,512]{2,1,0:T(2,128)(2,1)}), bf16[8,2,512]{2,1,0:T(2,128)(2,1)S(1)}, u32[]{:S(2)}, u32[]{:S(2)}) async-start(bf16[8,2,512]{2,1,0:T(2,128)(2,1)} %reshape.506), calls=%async_computation.1 | async-start | bytes 32768 | tf_op jit(solution)/shard_map/all_to_all | solution.py:107
  199.1 14.8 %fusion.11 = bf16[8,128,4,256]{3,1,2,0:T(8,128)(2,1)S(1)} fusion(f32[8,128,4,256]{3,1,2,0:T(8,128)} %fusion.21, bf16[1024,8,128,1]{0,2,3,1:T(8,128)(2,1)} %bitcast.165, f32[8,256,4,1024]{3,1,2,0:T(8,128)} %get-tuple-element.18, f32[8,4,256]{2,1,0:T(4,128)S(1)} %get-tuple-element.6, pred[1024]{0:T(1024)(128)(4,1)S(1)} %add_compare_fusion), kind=kOutput, calls=%fused_computation.16 | convolution fusion | flops 2183135232 | bytes 41976832 | tf_op jit(solution)/shard_map/sagcw,swah->scagh/dot_general | solution.py:84
  213.9 7.9 %copy.55 = bf16[1,1,256,4096]{3,1,0,2:T(2,128)(2,1)} copy(bf16[1,1,256,4096]{2,3,1,0:T(8,128)(2,1)S(1)} %bitcast.164) | data formatting | bytes 4194304 | tf_op jit(solution)/shard_map/convert_element_type | solution.py:101
  221.8 13.4 %reduce.12 = bf16[256,4096]{1,0:T(8,128)(2,1)S(1)} reduce(bf16[256,1,1,4096]{3,2,1,0:T(2,128)(2,1)} %bitcast.157, bf16[]{:T(256)} %broadcast.177), dimensions={1,2}, to_apply=%bitcast.136.reduce_sub_computation | reduce | bytes 4194306
  235.2 3.8 %reshape.504 = bf16[8,2,65536]{2,1,0:T(2,128)(2,1)} reshape(bf16[256,4096]{1,0:T(8,128)(2,1)S(1)} %reduce.12) | data formatting | bytes 4194304
  239.0 5.1 %all-to-all-start.2 = ((bf16[8,2,65536]{2,1,0:T(2,128)(2,1)}), bf16[8,2,65536]{2,1,0:T(2,128)(2,1)S(1)}, u32[]{:S(2)}, u32[]{:S(2)}) async-start(bf16[8,2,65536]{2,1,0:T(2,128)(2,1)} %reshape.504), calls=%async_computation.2 | async-start | bytes 4194304 | tf_op jit(solution)/shard_map/all_to_all | solution.py:100
  245.4 47.7 %all-to-all-done.2 = bf16[8,2,65536]{2,1,0:T(2,128)(2,1)S(1)} async-done(((bf16[8,2,65536]{2,1,0:T(2,128)(2,1)}), bf16[8,2,65536]{2,1,0:T(2,128)(2,1)S(1)}, u32[]{:S(2)}, u32[]{:S(2)}) %all-to-all-start.2) | async-done | bytes 2097184 | tf_op jit(solution)/shard_map/all_to_all | solution.py:100
  293.2 4.4 %reshape.505 = bf16[256,1,1,4096]{3,2,1,0:T(2,128)(2,1)} reshape(bf16[8,2,65536]{2,1,0:T(2,128)(2,1)S(1)} %all-to-all-done.2) | data formatting | bytes 4194304
  297.6 6.6 %bitcast_convert_fusion = f32[1,1,256,4096]{3,1,0,2:T(1,128)S(1)} fusion(bf16[256,1,1,4096]{3,2,1,0:T(2,128)(2,1)} %reshape.505), kind=kLoop, calls=%fused_computation.69 | loop fusion | flops 1048576 | bytes 6291456 | tf_op jit(solution)/shard_map/convert_element_type | solution.py:106
  (57 shorter events, 12.5 us)
Async XLA Ops:
  6.5 114.2 %copy-start = (bf16[2,4096,128]{2,1,0:T(8,128)(2,1)S(1)}, bf16[2,4096,128]{2,1,0:T(8,128)(2,1)}, u32[]{:S(2)}) copy-start(bf16[2,4096,128]{2,1,0:T(8,128)(2,1)} %param.12) | copy-start | bytes 6291460
  6.5 146.3 %all-gather.2.cloned.1.call-start = ((), (), s32[]{:S(2)}) async-start(), calls=%async_computation.4 | async-start | bytes 2359296 | tf_op jit(solution)/shard_map/all_gather | solution.py:61
  124.5 13.9 %all-to-all-start = ((bf16[2,256,1,128]{3,0,2,1:T(2,128)(2,1)}), bf16[2,256,1,128]{3,0,2,1:T(2,128)(2,1)S(1)}, u32[]{:S(2)}, u32[]{:S(2)}) async-start(bf16[2,256,1,128]{3,0,2,1:T(2,128)(2,1)} %copy.48), calls=%async_computation | async-start | bytes 262144 | tf_op jit(solution)/shard_map/all_to_all | solution.py:55
  152.8 15.7 %copy-start.2 = (bf16[256,1,4096]{0,2,1:T(8,128)(2,1)S(1)}, bf16[256,1,4096]{0,2,1:T(8,128)(2,1)}, u32[]{:S(2)}) copy-start(bf16[256,1,4096]{0,2,1:T(8,128)(2,1)} %all-gather.2.cloned.1.call-done) | copy-start | bytes 6291460
  186.2 8.9 %all-to-all-start.3 = ((bf16[8,2,512]{2,1,0:T(2,128)(2,1)}), bf16[8,2,512]{2,1,0:T(2,128)(2,1)S(1)}, u32[]{:S(2)}, u32[]{:S(2)}) async-start(bf16[8,2,512]{2,1,0:T(2,128)(2,1)} %reshape.508), calls=%async_computation.3 | async-start | bytes 32768 | tf_op jit(solution)/shard_map/all_to_all | solution.py:110
  195.1 44.0 %all-to-all-start.1 = ((bf16[8,2,512]{2,1,0:T(2,128)(2,1)}), bf16[8,2,512]{2,1,0:T(2,128)(2,1)S(1)}, u32[]{:S(2)}, u32[]{:S(2)}) async-start(bf16[8,2,512]{2,1,0:T(2,128)(2,1)} %reshape.506), calls=%async_computation.1 | async-start | bytes 32768 | tf_op jit(solution)/shard_map/all_to_all | solution.py:107
  239.0 54.1 %all-to-all-start.2 = ((bf16[8,2,65536]{2,1,0:T(2,128)(2,1)}), bf16[8,2,65536]{2,1,0:T(2,128)(2,1)S(1)}, u32[]{:S(2)}, u32[]{:S(2)}) async-start(bf16[8,2,65536]{2,1,0:T(2,128)(2,1)} %reshape.504), calls=%async_computation.2 | async-start | bytes 4194304 | tf_op jit(solution)/shard_map/all_to_all | solution.py:100
  297.6 9.1 %copy-start.1 = (bf16[2,4096,128]{2,1,0:T(8,128)(2,1)S(1)}, bf16[2,4096,128]{2,1,0:T(8,128)(2,1)}, u32[]{:S(2)}) copy-start(bf16[2,4096,128]{2,1,0:T(8,128)(2,1)} %param.12) | copy-start | bytes 6291460
Sparse Core Ops, SparseCore 0:
  120.9 31.9 all-gather.1
where the time goes:
time: 314 us
  blocking collectives  90.9 us (29%)
  waiting for transfers between devices  63 us (20%)
  matrix products  48.8 us (16%)
  other arithmetic  43.2 us (14%)
  local copies, waits for them, and re-layouts  36.5 us (12%)
  starting transfers between devices  16 us (5%)
  between operations  15.1 us (5%)
    psum x1, blocking collectives, body(): lax.psum(jnp.einsum('sci,id->csd', gen_hidden, out_proj, preferred_elemen...  90.9 us
    all_to_all x1, waiting for transfers between devices, body(): lax.all_to_all(partial_value.astype(jnp.bfloat16), ('seq', 'sub'), split_...  47.7 us
    dot_general x1, matrix products, body(): jnp.einsum('csagh,swah->sagcw', grouped, cached[0], preferred_element_typ...  15.6 us
    unnamed x3, other arithmetic  15.3 us
    reduce_sum x2, other arithmetic, body(): total = jnp.sum(cache_weights, axis=-1) + jnp.sum(span_weights, axis=-1)  14.9 us
    dot_general x1, matrix products, body(): jnp.einsum('sagcw,swah->scagh', cache_weights.astype(jnp.bfloat16), cache...  14.8 us
    all_gather x1, waiting for transfers between devices, body(): lax.all_gather(query.reshape(span, sessions, local_heads * HD), ('seq', '...  14.2 us
    unnamed x14, local copies, waits for them, and re-layouts  13.2 us
  transfers between devices with their start and end apart: 5, of which 3 were waited for; matrix products, arithmetic and copies ran while one was open for 19% of the time, Pallas kernels for 0%

commit v1 on v0

--- a/solution.py
+++ b/solution.py
@@ -1,8 +1,11 @@
+import functools
 import math
 
 import jax
 import jax.numpy as jnp
 from jax import lax
+from jax.experimental import pallas as pl
+from jax.experimental.pallas import tpu as pltpu
 from jax.sharding import PartitionSpec as P
 
 QH = 32
@@ -118,6 +121,469 @@
     return (numer / denom[..., None]).astype(jnp.bfloat16).reshape(sessions, rows, QH * HD)
 
 
+MESH = pl.DeviceIdType.MESH
+CHUNKS = 4
+BF = jnp.bfloat16
+F32 = jnp.float32
+
+
+def fused_kernel(
+    shards_z,
+    hid,
+    wo,
+    gain,
+    wq,
+    wkv,
+    cache,
+    lengths,
+    cosf,
+    sinf,
+    out,
+    hid_v,
+    wo_v,
+    w_v,
+    k_v,
+    v_v,
+    p_send,
+    p_recv,
+    own_part,
+    rs_send,
+    rs_recv,
+    x_all,
+    acc,
+    ssq,
+    q_all,
+    kn,
+    vn,
+    o_send,
+    o_recv,
+    fin,
+    f_recv,
+    in_sem,
+    wo_sem,
+    kvl_sem,
+    kvs_sem,
+    kvr_sem,
+    ps_sem,
+    pr_sem,
+    rss_sem,
+    rsr_sem,
+    ags_sem,
+    agr_sem,
+    fws_sem,
+    fwr_sem,
+    qs_sem,
+    qr_sem,
+    os_sem,
+    or_sem,
+    fs_sem,
+    fr_sem,
+):
+    Z = shards_z
+    z = lax.axis_index("seq")
+    c = lax.axis_index("sub")
+    other = 1 - c
+    rows = hid.shape[2]
+    span = 2 * Z * rows
+    width = wo.shape[1]
+    cw = width // CHUNKS
+    ql = wq.shape[1]
+    heads = ql // HD
+    wl = cache.shape[1]
+    tile = 256
+    partner = {"seq": z, "sub": other}
+
+    def peer(d):
+        return lax.rem(z + d, Z)
+
+    def remote(src, dst, ss, rs, zz, cc):
+        return pltpu.make_async_remote_copy(
+            src_ref=src,
+            dst_ref=dst,
+            send_sem=ss,
+            recv_sem=rs,
+            device_id={"seq": zz, "sub": cc},
+            device_id_type=MESH,
+        )
+
+    def hid_copy():
+        return pltpu.make_async_copy(hid, hid_v, in_sem.at[0])
+
+    def wo_copy(k):
+        return pltpu.make_async_copy(
+            wo.at[:, pl.ds(pl.multiple_of(k * cw, cw), cw)], wo_v.at[k], wo_sem.at[k]
+        )
+
+    def w_copies():
+        return (
+            pltpu.make_async_copy(wq, w_v.at[:, 0:ql], in_sem.at[1]),
+            pltpu.make_async_copy(wkv.at[0], w_v.at[:, ql : ql + HD], in_sem.at[2]),
+            pltpu.make_async_copy(wkv.at[1], w_v.at[:, ql + HD : ql + 2 * HD], in_sem.at[3]),
+        )
+
+    def kv_src(i, j, cc):
+        return cache.at[i, :, pl.ds(pl.multiple_of((2 * j + cc) * HD, HD), HD)]
+
+    def kv_dst(i, j):
+        return (k_v, v_v)[i].at[j, pl.ds(pl.multiple_of(c * wl, wl), wl), :]
+
+    def kv_local(i, j):
+        return pltpu.make_async_copy(kv_src(i, j, c), kv_dst(i, j), kvl_sem.at[i, j])
+
+    def kv_remote(i, j):
+        return remote(
+            kv_src(i, j, other), kv_dst(i, j), kvs_sem.at[i, j], kvr_sem.at[i, j], z, other
+        )
+
+    def pair_copy(k):
+        return remote(p_send.at[k], p_recv.at[k], ps_sem.at[k], pr_sem.at[k], z, other)
+
+    def rs_copy(k, d):
+        return remote(
+            rs_send.at[k, peer(d)],
+            rs_recv.at[k, d],
+            rss_sem.at[k, d],
+            rsr_sem.at[k, d],
+            peer(d),
+            c,
+        )
+
+    mine = 2 * z + c
+
+    def ag_copy(k, d):
+        return remote(
+            x_all.at[k, mine], x_all.at[k, mine], ags_sem.at[k, d], agr_sem.at[k, d], peer(d), c
+        )
+
+    def fw_copy(k, d):
+        blk = x_all.at[k, 2 * lax.rem(z + Z - d, Z) + c]
+        return remote(blk, blk, fws_sem.at[k, d], fwr_sem.at[k, d], z, other)
+
+    def q_copy(d):
+        return remote(q_all.at[z], q_all.at[z], qs_sem.at[d], qr_sem.at[d], peer(d), c)
+
+    def o_copy(j, d):
+        return remote(
+            o_send.at[j, pl.ds(pl.multiple_of(peer(d) * 2 * rows, 2 * rows), 2 * rows), :],
+            o_recv.at[d, j],
+            os_sem.at[j, d],
+            or_sem.at[j, d],
+            peer(d),
+            c,
+        )
+
+    def f_copy():
+        src = fin.at[:, pl.ds(pl.multiple_of(other * rows, rows), rows), :]
+        return remote(src, f_recv, fs_sem.at[0], fr_sem.at[0], z, other)
+
+    hid_copy().start()
+    for k in range(CHUNKS):
+        wo_copy(k).start()
+    barrier = pltpu.get_barrier_semaphore()
+    for d in range(1, Z):
+        pl.semaphore_signal(
+            barrier, inc=1, device_id={"seq": peer(d), "sub": c}, device_id_type=MESH
+        )
+    pl.semaphore_signal(barrier, inc=1, device_id=partner, device_id_type=MESH)
+    pl.semaphore_wait(barrier, Z)
+
+    hid_copy().wait()
+    ssq[...] = jnp.zeros_like(ssq)
+    acc[...] = jnp.zeros_like(acc)
+
+    def part(k, cc, store):
+        lhs = hid_v[:, pl.ds(cc, 1)].reshape(Z * rows, hid.shape[3])
+
+        def go(t, carry):
+            cols = pl.ds(pl.multiple_of(t * tile, tile), tile)
+            store(cols, jnp.dot(lhs, wo_v[k, :, cols], preferred_element_type=F32))
+            return carry
+
+        lax.fori_loop(0, cw // tile, go, 0)
+
+    def pair_sum(k):
+        pair_copy(k).wait_recv()
+        both = own_part[k] + p_recv[k].astype(F32)
+        rs_send[k] = both.astype(BF).reshape(Z, rows, cw)
+        for d in range(1, Z):
+            rs_copy(k, d).start()
+
+    def stage_a(k, carry):
+        wo_copy(k).wait()
+
+        def store_p(cols, value):
+            p_send[k, :, cols] = value.astype(BF)
+
+        def store_m(cols, value):
+            own_part[k, :, cols] = value
+
+        part(k, other, store_p)
+        pair_copy(k).start()
+        part(k, c, store_m)
+
+        @pl.when(k >= 1)
+        def _():
+            pair_sum(k - 1)
+
+        return carry
+
+    lax.fori_loop(0, CHUNKS, stage_a, 0)
+    pair_sum(CHUNKS - 1)
+
+    for copy in w_copies():
+        copy.start()
+    for i in range(2):
+        for j in range(Z):
+            kv_local(i, j).start()
+            kv_remote(i, j).start()
+
+    def stage_c(k, carry):
+        total = rs_send[k, z].astype(F32)
+        for d in range(1, Z):
+            rs_copy(k, d).wait_recv()
+            total = total + rs_recv[k, d].astype(F32)
+        x_all[k, mine] = total.astype(BF)
+        for d in range(1, Z):
+            ag_copy(k, d).start()
+        fw_copy(k, 0).start()
+        return carry
+
+    lax.fori_loop(0, CHUNKS, stage_c, 0)
+    for copy in w_copies():
+        copy.wait()
+
+    def ag_wait(k, d):
+        src = x_all.at[k, 2 * lax.rem(z + Z - d, Z) + c]
+        remote(src, src, ags_sem.at[k, d], agr_sem.at[k, d], peer(d), c).wait_recv()
+
+    def fw_wait(k, d):
+        src = x_all.at[k, 2 * lax.rem(z + Z - d, Z) + other]
+        remote(src, src, fws_sem.at[k, d], fwr_sem.at[k, d], z, other).wait_recv()
+
+    def stage_d(k, carry):
+        for d in range(1, Z):
+            ag_wait(k, d)
+            fw_copy(k, d).start()
+        for d in range(Z):
+            fw_wait(k, d)
+        x = x_all[k].reshape(span, cw).astype(F32)
+        ssq[...] += jnp.sum(x * x, axis=-1, keepdims=True)
+        cols = pl.ds(pl.multiple_of(k * cw, cw), cw)
+        xg = (x * gain[:, cols].astype(F32)).astype(BF)
+        acc[...] += jnp.dot(xg, w_v[cols, :], preferred_element_type=F32)
+        return carry
+
+    lax.fori_loop(0, CHUNKS, stage_d, 0)
+
+    inverse = lax.rsqrt(ssq[...] * (1.0 / width) + EPS)
+    cosine = cosf[...]
+    sine = sinf[...]
+
+    def rope(value):
+        return value * cosine + pltpu.roll(value, HD // 2, 1) * sine
+
+    for h in range(heads):
+        value = acc[:, h * HD : (h + 1) * HD] * inverse
+        q_all[z, :, h * HD : (h + 1) * HD] = rope(value).astype(BF)
+    for d in range(1, Z):
+        q_copy(d).start()
+    key_raw = (acc[:, ql : ql + HD] * inverse).astype(BF)
+    kn[...] = rope(key_raw.astype(F32)).astype(BF)
+    vn[...] = (acc[:, ql + HD : ql + 2 * HD] * inverse).astype(BF)
+
+    for i in range(2):
+        for j in range(Z):
+            kv_local(i, j).wait()
+            kv_remote(i, j).wait_recv()
+
+    length = lengths[0]
+    slots = z * 2 * wl + lax.broadcasted_iota(jnp.int32, (1, 2 * wl), 1)
+    live = slots < length
+    c2 = math.log2(math.e) / math.sqrt(HD)
+    nt = (((1,), (1,)), ((), ()))
+    lane = lax.broadcasted_iota(jnp.int32, (span, HD), 1)
+
+    def attend(j, own):
+        def head(h, stats):
+            cols = pl.ds(pl.multiple_of(h * HD, HD), HD)
+            q = q_all[j, :, cols]
+            s = lax.dot_general(q, k_v[j], nt, preferred_element_type=F32)
+            s = jnp.where(live, s, NEG)
+            top = jnp.max(s, axis=-1, keepdims=True)
+            if own:
+                s2 = lax.dot_general(q, kn[...], nt, preferred_element_type=F32)
+                r = lax.broadcasted_iota(jnp.int32, (span, span), 0)
+                t = lax.broadcasted_iota(jnp.int32, (span, span), 1)
+                s2 = jnp.where(t <= r, s2, NEG)
+                top = jnp.maximum(top, jnp.max(s2, axis=-1, keepdims=True))
+            top = top * c2
+            p = jnp.exp2(s * c2 - top)
+            total = jnp.sum(p, axis=-1, keepdims=True)
+            mixed = jnp.dot(p.astype(BF), v_v[j], preferred_element_type=F32)
+            if own:
+                p2 = jnp.exp2(s2 * c2 - top)
+                total = total + jnp.sum(p2, axis=-1, keepdims=True)
+                mixed = mixed + jnp.dot(p2.astype(BF), vn[...], preferred_element_type=F32)
+            o_send[j, :, cols] = (mixed * (1.0 / total)).astype(BF)
+            lse = top + jnp.log2(total)
+            return jnp.where((lane == h) | (lane == h + heads), lse, stats)
+
+        stats = lax.fori_loop(0, heads, head, jnp.zeros((span, HD), F32))
+        high = stats.astype(BF)
+        low = (stats - high.astype(F32)).astype(BF)
+        o_send[j, :, ql : ql + HD] = jnp.where(lane < heads, high.astype(F32), low.astype(F32)).astype(BF)
+        for d in range(1, Z):
+            o_copy(j, d).start()
+        o_recv[0, j] = o_send[j, pl.ds(pl.multiple_of(z * 2 * rows, 2 * rows), 2 * rows), :]
+
+    attend(z, True)
+
+    def others(d, carry):
+        j = lax.rem(z + Z - d, Z)
+        remote(q_all.at[j], q_all.at[j], qs_sem.at[d], qr_sem.at[d], z, other).wait_recv()
+        attend(j, False)
+        return carry
+
+    lax.fori_loop(1, Z, others, 0)
+
+    def combine(j, carry):
+        for d in range(1, Z):
+            o_copy(j, d).wait_recv()
+        stats = []
+        for d in range(Z):
+            both = o_recv[d, j, :, ql : ql + HD].astype(F32)
+            stats.append(both + pltpu.roll(both, HD - heads, 1))
+        best = functools.reduce(jnp.maximum, stats)
+        shares = [jnp.exp2(s - best) for s in stats]
+        inv = 1.0 / functools.reduce(lambda a, b: a + b, shares)
+        shares = [s * inv for s in shares]
+        for h in range(heads):
+            cols = slice(h * HD, (h + 1) * HD)
+            mix = None
+            for d in range(Z):
+                term = shares[d][:, h : h + 1] * o_recv[d, j, :, cols].astype(F32)
+                mix = term if mix is None else mix + term
+            fin[j, :, cols] = mix.astype(BF)
+        return carry
+
+    lax.fori_loop(0, Z, combine, 0)
+    f_copy().start()
+    keep = pl.ds(pl.multiple_of(c * rows, rows), rows)
+    for j in range(Z):
+        out[0, :, pl.ds(pl.multiple_of((2 * j + c) * ql, ql), ql)] = fin[j, keep, :]
+    f_copy().wait_recv()
+    for j in range(Z):
+        out[0, :, pl.ds(pl.multiple_of((2 * j + other) * ql, ql), ql)] = f_recv[j]
+
+    f_copy().wait_send()
+    for i in range(2):
+        for j in range(Z):
+            kv_remote(i, j).wait_send()
+
+    def drain(k, carry):
+        pair_copy(k).wait_send()
+        for d in range(1, Z):
+            rs_copy(k, d).wait_send()
+            ag_copy(k, d).wait_send()
+        for d in range(Z):
+            fw_copy(k, d).wait_send()
+        return carry
+
+    lax.fori_loop(0, CHUNKS, drain, 0)
+    for d in range(1, Z):
+        q_copy(d).wait_send()
+
+    def drain_o(j, carry):
+        for d in range(1, Z):
+            o_copy(j, d).wait_send()
+        return carry
+
+    lax.fori_loop(0, Z, drain_o, 0)
+
+
+def fused(gen_hidden, out_proj, norm_gain, q_weight, kv_weight, kv_cache, lengths, span_start):
+    Z = lax.axis_size("seq")
+    _, span, dl = gen_hidden.shape
+    rows = span // (2 * Z)
+    width = out_proj.shape[1]
+    cw = width // CHUNKS
+    ql = q_weight.shape[1]
+    wl = kv_cache.shape[2]
+    half = HD // 2
+    freq = THETA ** (-jnp.arange(half, dtype=F32) * 2.0 / HD)
+    positions = span_start[0] + jnp.arange(span, dtype=jnp.int32)
+    angle = positions.astype(F32)[:, None] * freq
+    cosine = jnp.cos(angle)
+    sine = jnp.sin(angle)
+    cosf = jnp.concatenate([cosine, cosine], axis=-1)
+    sinf = jnp.concatenate([-sine, sine], axis=-1)
+    any_spec = pl.BlockSpec(memory_space=pl.ANY)
+    vm_spec = pl.BlockSpec(memory_space=pltpu.VMEM)
+    sm_spec = pl.BlockSpec(memory_space=pltpu.SMEM)
+    dma = pltpu.SemaphoreType.DMA
+    V = pltpu.VMEM
+    return pl.pallas_call(
+        functools.partial(fused_kernel, Z),
+        out_shape=jax.ShapeDtypeStruct((1, rows, 2 * Z * ql), BF),
+        in_specs=[any_spec, any_spec, vm_spec, any_spec, any_spec, any_spec, sm_spec, vm_spec, vm_spec],
+        out_specs=vm_spec,
+        scratch_shapes=[
+            V((Z, 2, rows, dl), BF),
+            V((CHUNKS, dl, cw), BF),
+            V((width, ql + 2 * HD), BF),
+            V((Z, 2 * wl, HD), BF),
+            V((Z, 2 * wl, HD), BF),
+            V((CHUNKS, Z * rows, cw), BF),
+            V((CHUNKS, Z * rows, cw), BF),
+            V((CHUNKS, Z * rows, cw), F32),
+            V((CHUNKS, Z, rows, cw), BF),
+            V((CHUNKS, Z, rows, cw), BF),
+            V((CHUNKS, 2 * Z, rows, cw), BF),
+            V((span, ql + 2 * HD), F32),
+            V((span, 1), F32),
+            V((Z, span, ql), BF),
+            V((span, HD), BF),
+            V((span, HD), BF),
+            V((Z, span, ql + HD), BF),
+            V((Z, Z, 2 * rows, ql + HD), BF),
+            V((Z, 2 * rows, ql), BF),
+            V((Z, rows, ql), BF),
+            dma((4,)),
+            dma((CHUNKS,)),
+            dma((2, Z)),
+            dma((2, Z)),
+            dma((2, Z)),
+            dma((CHUNKS,)),
+            dma((CHUNKS,)),
+            dma((CHUNKS, Z)),
+            dma((CHUNKS, Z)),
+            dma((CHUNKS, Z)),
+            dma((CHUNKS, Z)),
+            dma((CHUNKS, Z)),
+            dma((CHUNKS, Z)),
+            dma((Z,)),
+            dma((Z,)),
+            dma((Z, Z)),
+            dma((Z, Z)),
+            dma((1,)),
+            dma((1,)),
+        ],
+        compiler_params=pltpu.CompilerParams(
+            collective_id=0, has_side_effects=True, vmem_limit_bytes=64000000
+        ),
+    )(
+        gen_hidden.reshape(Z, 2, rows, dl),
+        out_proj,
+        norm_gain.reshape(1, width),
+        q_weight,
+        kv_weight,
+        kv_cache.reshape(2, wl, KVH * HD),
+        lengths,
+        cosf,
+        sinf,
+    )
+
+
 def solution(mesh):
     placed = (
         P(("groups", "batch"), None, ("seq", "sub")),
@@ -129,8 +595,9 @@
         P(("groups", "batch")),
         P(("groups", "batch")),
     )
+    aligned = mesh.shape["sub"] == 2 and mesh.shape["seq"] * 2 == KVH
     return jax.shard_map(
-        body,
+        fused if aligned else body,
         mesh=mesh,
         in_specs=placed,
         out_specs=P(("groups", "batch"), ("seq", "sub"), None),

time: 314 us -> 120 us (0.38)
  Pallas kernels: 0 us -> 114 us
  blocking collectives: 90.9 us -> 0 us
  waiting for transfers between devices: 63 us -> 0 us
  matrix products: 48.8 us -> 0 us
  other arithmetic: 43.2 us -> 1.39 us
  local copies, waits for them, and re-layouts: 36.5 us -> 2.98 us
  starting transfers between devices: 16 us -> 0 us
  between operations: 15.1 us -> 1.33 us
    pallas_call x0 -> x1, Pallas kernels: none -> 114 us  [fused(): pl.pallas_call(functools.partial(fused_kernel, Z), out_shape=jax.ShapeDty...]
    psum x1 -> x0, blocking collectives: 90.9 us -> none  [body(): lax.psum(jnp.einsum('sci,id->csd', gen_hidden, out_proj, preferred_elemen...]
    dot_general x7 -> x0, matrix products: 48.8 us -> none  [the longest x1 15.6 us: body(): jnp.einsum('csagh,swah->sagcw', grouped, cached[0], preferred_element_typ...]
    all_to_all x4 -> x0, waiting for transfers between devices: 48.7 us -> none  [the longest x1 47.7 us: body(): lax.all_to_all(partial_value.astype(jnp.bfloat16), ('seq', 'sub'), split_...]
    reduce_sum x5 -> x0, other arithmetic: 18.5 us -> none  [the longest x2 14.9 us: body(): total = jnp.sum(cache_weights, axis=-1) + jnp.sum(span_weights, axis=-1)]
    all_to_all x4 -> x0, starting transfers between devices: 16 us -> none  [the longest x1 5.08 us: body(): lax.all_to_all(partial_value.astype(jnp.bfloat16), ('seq', 'sub'), split_...]
    unnamed x3 -> x0, other arithmetic: 15.3 us -> none
    all_gather x1 -> x0, waiting for transfers between devices: 14.2 us -> none  [body(): lax.all_gather(query.reshape(span, sessions, local_heads * HD), ('seq', '...]
  transfers between devices with their start and end apart: 5 -> 0, of which waited for: 3 -> 0; matrix products, arithmetic and copies ran while one was open for 19% -> 0% of each run, Pallas kernels for 0% -> 0%
where the time goes in v1:
time: 120 us
  Pallas kernels  114 us (95%)
  local copies, waits for them, and re-layouts  2.98 us (2%)
  other arithmetic  1.39 us (1%)
  between operations  1.33 us (1%)
    pallas_call x1, Pallas kernels, fused(): pl.pallas_call(functools.partial(fused_kernel, Z), out_shape=jax.ShapeDty...  114 us

profile of v1, /device:TPU:0, one launch (start us, length us, event | category | flops | bytes accessed | tf_op | source)
XLA Modules:
  0.0 119.7 jit_solution(15963606225789736403)
XLA Ops:
  0.7 0.5 fusion
  1.2 0.8 pad_maximum_fusion
  2.1 1.3 %reshape.21.gain = bf16[1,4096]{1,0:T(2,128)(2,1)} reshape(bf16[4096]{0:T(1024)(128)(2,1)} %param.10) | data formatting | bytes 16384 | tf_op jit(solution)/shard_map/reshape | solution.py:577
  4.0 114.0 %shard_map.82 = bf16[1,32,4096]{2,1,0:T(8,128)(2,1)} custom-call(bf16[4,2,32,1024]{3,2,1,0:T(8,128)(2,1)} %bitcast.5, bf16[1024,4096]{1,0:T(8,128)(2,1)} %wo.1, bf16[1,4096]{1,0:T(2,128)(2,1)} %reshape.21.gain, bf16[4096,512]{1,0:T(8,128)(2,1)} %wq.1, bf16[2,4096,128]{2,1,0:T(8,128)(2,1)} %wkv.1, bf16[2,1024,1024]{2,1,0:T(8,128)(2,1)} %bitcast.4, ...), custom_call_target="tpu_custom_call" | custom-call | tf_op jit(solution)/shard_map/pallas_call | solution.py:525
  118.0 1.7 %copy.12 = bf16[1,32,4096]{2,1,0:T(8,128)(2,1)} copy(bf16[1,32,4096]{2,1,0:T(8,128)(2,1)} %shard_map.82) | data formatting | bytes 524288
  (2 shorter events, 0.0 us)

commit v2 on v1

--- a/solution.py
+++ b/solution.py
@@ -149,6 +149,7 @@
     own_part,
     rs_send,
     rs_recv,
+    rs_merged,
     x_all,
     acc,
     ssq,
@@ -157,6 +158,7 @@
     vn,
     o_send,
     o_recv,
+    o_merged,
     fin,
     f_recv,
     in_sem,
@@ -193,8 +195,14 @@
     tile = 256
     partner = {"seq": z, "sub": other}
 
-    def peer(d):
-        return lax.rem(z + d, Z)
+    inner = (z == 1) | (z == 2)
+    near = z + 1 - 2 * lax.rem(z, 2)
+    far_in = jnp.where(z < 2, 2, 1)
+    far_out = jnp.where(z < 2, 3, 0)
+    group_at = (z, near, far_in, far_out)
+    my_in = jnp.where(z < 2, 1, 2)
+    my_out = jnp.where(z < 2, 0, 3)
+    merge_order = (my_out, my_in, far_in, far_out)
 
     def remote(src, dst, ss, rs, zz, cc):
         return pltpu.make_async_remote_copy(
@@ -207,7 +215,10 @@
         )
 
     def hid_copy():
-        return pltpu.make_async_copy(hid, hid_v, in_sem.at[0])
+        return (
+            pltpu.make_async_copy(hid.at[:, other], hid_v.at[0], in_sem.at[0]),
+            pltpu.make_async_copy(hid.at[:, c], hid_v.at[1], in_sem.at[4]),
+        )
 
     def wo_copy(k):
         return pltpu.make_async_copy(
@@ -238,37 +249,62 @@
     def pair_copy(k):
         return remote(p_send.at[k], p_recv.at[k], ps_sem.at[k], pr_sem.at[k], z, other)
 
-    def rs_copy(k, d):
+    mine = 2 * z + c
+
+    def rs_copy(k, slot, who):
         return remote(
-            rs_send.at[k, peer(d)],
-            rs_recv.at[k, d],
-            rss_sem.at[k, d],
-            rsr_sem.at[k, d],
-            peer(d),
+            rs_send.at[k, who],
+            rs_recv.at[k, slot],
+            rss_sem.at[k, slot],
+            rsr_sem.at[k, slot],
+            near,
             c,
         )
 
-    mine = 2 * z + c
-
-    def ag_copy(k, d):
+    def rs_cross(k, which):
+        who = (far_in, far_out)[which]
         return remote(
-            x_all.at[k, mine], x_all.at[k, mine], ags_sem.at[k, d], agr_sem.at[k, d], peer(d), c
-        )
+            rs_merged.at[k, which],
+            rs_recv.at[k, 4],
+            rss_sem.at[k, 4 + which],
+            rsr_sem.at[k, 4],
+            who,
+            c,
+        )
+
+    def ag_copy(k, block, slot, sem, who):
+        blk = x_all.at[k, 2 * block + c]
+        return remote(blk, blk, ags_sem.at[k, sem], agr_sem.at[k, slot], who, c)
 
     def fw_copy(k, d):
-        blk = x_all.at[k, 2 * lax.rem(z + Z - d, Z) + c]
+        blk = x_all.at[k, 2 * group_at[d] + c]
         return remote(blk, blk, fws_sem.at[k, d], fwr_sem.at[k, d], z, other)
 
-    def q_copy(d):
-        return remote(q_all.at[z], q_all.at[z], qs_sem.at[d], qr_sem.at[d], peer(d), c)
-
-    def o_copy(j, d):
+    def q_copy(block, slot, sem, who):
+        blk = q_all.at[block]
+        return remote(blk, blk, qs_sem.at[sem], qr_sem.at[slot], who, c)
+
+    def chip_rows(who):
+        return pl.ds(pl.multiple_of(who * 2 * rows, 2 * rows), 2 * rows)
+
+    def o_copy(j, slot, who):
         return remote(
-            o_send.at[j, pl.ds(pl.multiple_of(peer(d) * 2 * rows, 2 * rows), 2 * rows), :],
-            o_recv.at[d, j],
-            os_sem.at[j, d],
-            or_sem.at[j, d],
-            peer(d),
+            o_send.at[j, chip_rows(who), :],
+            o_recv.at[slot, j],
+            os_sem.at[j, slot],
+            or_sem.at[j, slot],
+            near,
+            c,
+        )
+
+    def o_cross(j, which):
+        who = (far_in, far_out)[which]
+        return remote(
+            o_merged.at[j, which],
+            o_recv.at[4, j],
+            os_sem.at[j, 4 + which],
+            or_sem.at[j, 4],
+            who,
             c,
         )
 
@@ -276,50 +312,49 @@
         src = fin.at[:, pl.ds(pl.multiple_of(other * rows, rows), rows), :]
         return remote(src, f_recv, fs_sem.at[0], fr_sem.at[0], z, other)
 
-    hid_copy().start()
+    for copy in hid_copy():
+        copy.start()
     for k in range(CHUNKS):
         wo_copy(k).start()
     barrier = pltpu.get_barrier_semaphore()
-    for d in range(1, Z):
+    for who in (near, far_in, far_out):
         pl.semaphore_signal(
-            barrier, inc=1, device_id={"seq": peer(d), "sub": c}, device_id_type=MESH
+            barrier, inc=1, device_id={"seq": who, "sub": c}, device_id_type=MESH
         )
     pl.semaphore_signal(barrier, inc=1, device_id=partner, device_id_type=MESH)
     pl.semaphore_wait(barrier, Z)
 
-    hid_copy().wait()
+    for copy in hid_copy():
+        copy.wait()
     ssq[...] = jnp.zeros_like(ssq)
     acc[...] = jnp.zeros_like(acc)
-
-    def part(k, cc, store):
-        lhs = hid_v[:, pl.ds(cc, 1)].reshape(Z * rows, hid.shape[3])
-
-        def go(t, carry):
-            cols = pl.ds(pl.multiple_of(t * tile, tile), tile)
-            store(cols, jnp.dot(lhs, wo_v[k, :, cols], preferred_element_type=F32))
-            return carry
-
-        lax.fori_loop(0, cw // tile, go, 0)
 
     def pair_sum(k):
         pair_copy(k).wait_recv()
         both = own_part[k] + p_recv[k].astype(F32)
         rs_send[k] = both.astype(BF).reshape(Z, rows, cw)
-        for d in range(1, Z):
-            rs_copy(k, d).start()
+        rs_copy(k, 1, near).start()
+
+        @pl.when(jnp.logical_not(inner))
+        def _():
+            rs_copy(k, 2, far_in).start()
+            rs_copy(k, 3, far_out).start()
 
     def stage_a(k, carry):
         wo_copy(k).wait()
 
-        def store_p(cols, value):
-            p_send[k, :, cols] = value.astype(BF)
-
-        def store_m(cols, value):
-            own_part[k, :, cols] = value
-
-        part(k, other, store_p)
+        lhs = hid_v[...].reshape(span, hid.shape[3])
+        half = Z * rows
+
+        def go(t, carry):
+            cols = pl.ds(pl.multiple_of(t * tile, tile), tile)
+            value = jnp.dot(lhs, wo_v[k, :, cols], preferred_element_type=F32)
+            p_send[k, :, cols] = value[:half].astype(BF)
+            own_part[k, :, cols] = value[half:]
+            return carry
+
+        lax.fori_loop(0, cw // tile, go, 0)
         pair_copy(k).start()
-        part(k, c, store_m)
 
         @pl.when(k >= 1)
         def _():
@@ -337,33 +372,58 @@
             kv_local(i, j).start()
             kv_remote(i, j).start()
 
-    def stage_c(k, carry):
+    def merge_rs(k):
+        for which, who in ((0, far_in), (1, far_out)):
+            rs_copy(k, 2 + which, who).wait_recv()
+            both = rs_send[k, who].astype(F32) + rs_recv[k, 2 + which].astype(F32)
+            rs_merged[k, which] = both.astype(BF)
+            rs_cross(k, which).start()
+
+    def stage_c(k):
         total = rs_send[k, z].astype(F32)
-        for d in range(1, Z):
-            rs_copy(k, d).wait_recv()
-            total = total + rs_recv[k, d].astype(F32)
+        rs_copy(k, 1, near).wait_recv()
+        total = total + rs_recv[k, 1].astype(F32)
+        rs_cross(k, 0).wait_recv()
+        total = total + rs_recv[k, 4].astype(F32)
         x_all[k, mine] = total.astype(BF)
-        for d in range(1, Z):
-            ag_copy(k, d).start()
+        ag_copy(k, z, 1, 0, near).start()
+
+        @pl.when(inner)
+        def _():
+            ag_copy(k, z, 2, 1, far_in).start()
+
         fw_copy(k, 0).start()
-        return carry
-
-    lax.fori_loop(0, CHUNKS, stage_c, 0)
-    for copy in w_copies():
-        copy.wait()
-
-    def ag_wait(k, d):
-        src = x_all.at[k, 2 * lax.rem(z + Z - d, Z) + c]
-        remote(src, src, ags_sem.at[k, d], agr_sem.at[k, d], peer(d), c).wait_recv()
+
+    def ag_wait(k, slot):
+        ag_copy(k, group_at[slot], slot, 0, near).wait_recv()
 
     def fw_wait(k, d):
-        src = x_all.at[k, 2 * lax.rem(z + Z - d, Z) + other]
-        remote(src, src, fws_sem.at[k, d], fwr_sem.at[k, d], z, other).wait_recv()
-
-    def stage_d(k, carry):
-        for d in range(1, Z):
-            ag_wait(k, d)
-            fw_copy(k, d).start()
+        blk = x_all.at[k, 2 * group_at[d] + other]
+        remote(blk, blk, fws_sem.at[k, d], fwr_sem.at[k, d], z, other).wait_recv()
+
+    def stage_d(k):
+        ag_wait(k, 1)
+        fw_copy(k, 1).start()
+
+        @pl.when(inner)
+        def _():
+            ag_copy(k, near, 3, 2, far_in).start()
+
+        ag_wait(k, 2)
+        fw_copy(k, 2).start()
+
+        @pl.when(inner)
+        def _():
+            ag_copy(k, far_in, 2, 3, near).start()
+
+        ag_wait(k, 3)
+        fw_copy(k, 3).start()
+
+        @pl.when(inner)
+        def _():
+            ag_copy(k, far_out, 3, 4, near).start()
+
+    def stage_e(k):
         for d in range(Z):
             fw_wait(k, d)
         x = x_all[k].reshape(span, cw).astype(F32)
@@ -371,9 +431,32 @@
         cols = pl.ds(pl.multiple_of(k * cw, cw), cw)
         xg = (x * gain[:, cols].astype(F32)).astype(BF)
         acc[...] += jnp.dot(xg, w_v[cols, :], preferred_element_type=F32)
+
+    def staggered(step, carry):
+        @pl.when(inner & (step < CHUNKS))
+        def _():
+            merge_rs(step)
+
+        @pl.when((step >= 1) & (step < CHUNKS + 1))
+        def _():
+            stage_c(step - 1)
+
+        @pl.when((step >= 2) & (step < CHUNKS + 2))
+        def _():
+            stage_d(step - 2)
+
+        @pl.when(step == 3)
+        def _():
+            for copy in w_copies():
+                copy.wait()
+
+        @pl.when(step >= 3)
+        def _():
+            stage_e(step - 3)
+
         return carry
 
-    lax.fori_loop(0, CHUNKS, stage_d, 0)
+    lax.fori_loop(0, CHUNKS + 3, staggered, 0)
 
     inverse = lax.rsqrt(ssq[...] * (1.0 / width) + EPS)
     cosine = cosf[...]
@@ -385,8 +468,12 @@
     for h in range(heads):
         value = acc[:, h * HD : (h + 1) * HD] * inverse
         q_all[z, :, h * HD : (h + 1) * HD] = rope(value).astype(BF)
-    for d in range(1, Z):
-        q_copy(d).start()
+    q_copy(z, 1, 0, near).start()
+
+    @pl.when(inner)
+    def _():
+        q_copy(z, 2, 1, far_in).start()
+
     key_raw = (acc[:, ql : ql + HD] * inverse).astype(BF)
     kn[...] = rope(key_raw.astype(F32)).astype(BF)
     vn[...] = (acc[:, ql + HD : ql + 2 * HD] * inverse).astype(BF)
@@ -402,6 +489,11 @@
     c2 = math.log2(math.e) / math.sqrt(HD)
     nt = (((1,), (1,)), ((), ()))
     lane = lax.broadcasted_iota(jnp.int32, (span, HD), 1)
+
+    def packed_stats(stats, count):
+        high = stats.astype(BF).astype(F32)
+        lanes = lax.broadcasted_iota(jnp.int32, (count, HD), 1)
+        return jnp.where(lanes < heads, high, stats - high).astype(BF)
 
     def attend(j, own):
         def head(h, stats):
@@ -429,41 +521,85 @@
             return jnp.where((lane == h) | (lane == h + heads), lse, stats)
 
         stats = lax.fori_loop(0, heads, head, jnp.zeros((span, HD), F32))
-        high = stats.astype(BF)
-        low = (stats - high.astype(F32)).astype(BF)
-        o_send[j, :, ql : ql + HD] = jnp.where(lane < heads, high.astype(F32), low.astype(F32)).astype(BF)
-        for d in range(1, Z):
-            o_copy(j, d).start()
-        o_recv[0, j] = o_send[j, pl.ds(pl.multiple_of(z * 2 * rows, 2 * rows), 2 * rows), :]
-
-    attend(z, True)
-
-    def others(d, carry):
-        j = lax.rem(z + Z - d, Z)
-        remote(q_all.at[j], q_all.at[j], qs_sem.at[d], qr_sem.at[d], z, other).wait_recv()
-        attend(j, False)
-        return carry
-
-    lax.fori_loop(1, Z, others, 0)
-
-    def combine(j, carry):
-        for d in range(1, Z):
-            o_copy(j, d).wait_recv()
+        o_send[j, :, ql : ql + HD] = packed_stats(stats, span)
+        o_copy(j, 1, near).start()
+
+        @pl.when(jnp.logical_not(inner))
+        def _():
+            o_copy(j, 2, far_in).start()
+            o_copy(j, 3, far_out).start()
+
+    def joined(parts):
         stats = []
-        for d in range(Z):
-            both = o_recv[d, j, :, ql : ql + HD].astype(F32)
+        for p in parts:
+            both = p[:, ql : ql + HD].astype(F32)
             stats.append(both + pltpu.roll(both, HD - heads, 1))
         best = functools.reduce(jnp.maximum, stats)
         shares = [jnp.exp2(s - best) for s in stats]
-        inv = 1.0 / functools.reduce(lambda a, b: a + b, shares)
+        total = functools.reduce(lambda a, b: a + b, shares)
+        inv = 1.0 / total
         shares = [s * inv for s in shares]
+        mixes = []
         for h in range(heads):
             cols = slice(h * HD, (h + 1) * HD)
-            mix = None
-            for d in range(Z):
-                term = shares[d][:, h : h + 1] * o_recv[d, j, :, cols].astype(F32)
-                mix = term if mix is None else mix + term
-            fin[j, :, cols] = mix.astype(BF)
+            terms = [s[:, h : h + 1] * p[:, cols].astype(F32) for s, p in zip(shares, parts)]
+            mixes.append(functools.reduce(lambda a, b: a + b, terms).astype(BF))
+        return mixes, best + jnp.log2(total)
+
+    def merge_o(j):
+        for which, who in ((0, far_in), (1, far_out)):
+            o_copy(j, 2 + which, who).wait_recv()
+            mixes, lse = joined((o_send[j, chip_rows(who), :], o_recv[2 + which, j]))
+            for h in range(heads):
+                o_merged[j, which, :, h * HD : (h + 1) * HD] = mixes[h]
+            low = lax.broadcasted_iota(jnp.int32, lse.shape, 1) < heads
+            lse = jnp.where(low, lse, pltpu.roll(lse, heads, 1))
+            o_merged[j, which, :, ql : ql + HD] = packed_stats(lse, 2 * rows)
+            o_cross(j, which).start()
+
+    attend(z, True)
+
+    def q_wait(slot):
+        q_copy(group_at[slot], slot, 0, near).wait_recv()
+
+    q_wait(1)
+
+    @pl.when(inner)
+    def _():
+        q_copy(near, 3, 2, far_in).start()
+
+    def attend_others(slot, carry):
+        j = jnp.where(slot == 1, near, jnp.where(slot == 2, far_in, far_out))
+
+        @pl.when(slot >= 2)
+        def _():
+            blk = q_all.at[j]
+            remote(blk, blk, qs_sem.at[0], qr_sem.at[slot], near, c).wait_recv()
+
+            @pl.when(inner)
+            def _():
+                remote(blk, blk, qs_sem.at[slot + 1], qr_sem.at[slot], near, c).start()
+
+        attend(j, False)
+
+        @pl.when(inner)
+        def _():
+            merge_o(jnp.where(slot == 1, my_out, jnp.where(slot == 2, my_in, far_in)))
+
+        return carry
+
+    lax.fori_loop(1, Z, attend_others, 0)
+
+    @pl.when(inner)
+    def _():
+        merge_o(far_out)
+
+    def combine(j, carry):
+        o_copy(j, 1, near).wait_recv()
+        o_cross(j, 0).wait_recv()
+        mixes, _ = joined((o_send[j, chip_rows(z), :], o_recv[1, j], o_recv[4, j]))
+        for h in range(heads):
+            fin[j, :, h * HD : (h + 1) * HD] = mixes[h]
         return carry
 
     lax.fori_loop(0, Z, combine, 0)
@@ -480,22 +616,54 @@
         for j in range(Z):
             kv_remote(i, j).wait_send()
 
+    outer = jnp.logical_not(inner)
+
     def drain(k, carry):
         pair_copy(k).wait_send()
-        for d in range(1, Z):
-            rs_copy(k, d).wait_send()
-            ag_copy(k, d).wait_send()
+        rs_copy(k, 1, near).wait_send()
+        ag_copy(k, z, 1, 0, near).wait_send()
         for d in range(Z):
             fw_copy(k, d).wait_send()
+
+        @pl.when(outer)
+        def _():
+            rs_copy(k, 2, far_in).wait_send()
+            rs_copy(k, 3, far_out).wait_send()
+
+        @pl.when(inner)
+        def _():
+            rs_cross(k, 0).wait_send()
+            rs_cross(k, 1).wait_send()
+            ag_copy(k, z, 2, 1, far_in).wait_send()
+            ag_copy(k, near, 3, 2, far_in).wait_send()
+            ag_copy(k, far_in, 2, 3, near).wait_send()
+            ag_copy(k, far_out, 3, 4, near).wait_send()
+
         return carry
 
     lax.fori_loop(0, CHUNKS, drain, 0)
-    for d in range(1, Z):
-        q_copy(d).wait_send()
+    q_copy(z, 1, 0, near).wait_send()
+
+    @pl.when(inner)
+    def _():
+        q_copy(z, 2, 1, far_in).wait_send()
+        q_copy(near, 3, 2, far_in).wait_send()
+        q_copy(far_in, 2, 3, near).wait_send()
+        q_copy(far_out, 3, 4, near).wait_send()
 
     def drain_o(j, carry):
-        for d in range(1, Z):
-            o_copy(j, d).wait_send()
+        o_copy(j, 1, near).wait_send()
+
+        @pl.when(outer)
+        def _():
+            o_copy(j, 2, far_in).wait_send()
+            o_copy(j, 3, far_out).wait_send()
+
+        @pl.when(inner)
+        def _():
+            o_cross(j, 0).wait_send()
+            o_cross(j, 1).wait_send()
+
         return carry
 
     lax.fori_loop(0, Z, drain_o, 0)
@@ -528,7 +696,7 @@
         in_specs=[any_spec, any_spec, vm_spec, any_spec, any_spec, any_spec, sm_spec, vm_spec, vm_spec],
         out_specs=vm_spec,
         scratch_shapes=[
-            V((Z, 2, rows, dl), BF),
+            V((2, Z, rows, dl), BF),
             V((CHUNKS, dl, cw), BF),
             V((width, ql + 2 * HD), BF),
             V((Z, 2 * wl, HD), BF),
@@ -537,7 +705,8 @@
             V((CHUNKS, Z * rows, cw), BF),
             V((CHUNKS, Z * rows, cw), F32),
             V((CHUNKS, Z, rows, cw), BF),
-            V((CHUNKS, Z, rows, cw), BF),
+            V((CHUNKS, Z + 1, rows, cw), BF),
+            V((CHUNKS, 2, rows, cw), BF),
             V((CHUNKS, 2 * Z, rows, cw), BF),
             V((span, ql + 2 * HD), F32),
             V((span, 1), F32),
@@ -545,26 +714,27 @@
             V((span, HD), BF),
             V((span, HD), BF),
             V((Z, span, ql + HD), BF),
-            V((Z, Z, 2 * rows, ql + HD), BF),
+            V((Z + 1, Z, 2 * rows, ql + HD), BF),
+            V((Z, 2, 2 * rows, ql + HD), BF),
             V((Z, 2 * rows, ql), BF),
             V((Z, rows, ql), BF),
-            dma((4,)),
+            dma((5,)),
             dma((CHUNKS,)),
             dma((2, Z)),
             dma((2, Z)),
             dma((2, Z)),
             dma((CHUNKS,)),
             dma((CHUNKS,)),
+            dma((CHUNKS, 6)),
+            dma((CHUNKS, 5)),
+            dma((CHUNKS, 5)),
             dma((CHUNKS, Z)),
             dma((CHUNKS, Z)),
             dma((CHUNKS, Z)),
-            dma((CHUNKS, Z)),
-            dma((CHUNKS, Z)),
-            dma((CHUNKS, Z)),
+            dma((5,)),
             dma((Z,)),
-            dma((Z,)),
-            dma((Z, Z)),
-            dma((Z, Z)),
+            dma((Z, 6)),
+            dma((Z, 5)),
             dma((1,)),
             dma((1,)),
         ],

time: 120 us -> 113 us (0.942)
  Pallas kernels: 114 us -> 107 us
    pallas_call x1, Pallas kernels: 114 us -> 107 us  [fused(): pl.pallas_call(functools.partial(fused_kernel, Z), out_shape=jax.ShapeDty...]
where the time goes in v2:
time: 113 us
  Pallas kernels  107 us (95%)
  local copies, waits for them, and re-layouts  2.98 us (3%)
  other arithmetic  1.39 us (1%)
  between operations  1.33 us (1%)
    pallas_call x1, Pallas kernels, fused(): pl.pallas_call(functools.partial(fused_kernel, Z), out_shape=jax.ShapeDty...  107 us

profile of v2, /device:TPU:0, one launch (start us, length us, event | category | flops | bytes accessed | tf_op | source)
XLA Modules:
  0.0 112.9 jit_solution(15697764821881988814)
XLA Ops:
  0.7 0.5 fusion
  1.2 0.8 pad_maximum_fusion
  2.1 1.3 %reshape.21.gain = bf16[1,4096]{1,0:T(2,128)(2,1)} reshape(bf16[4096]{0:T(1024)(128)(2,1)} %param.10) | data formatting | bytes 16384 | tf_op jit(solution)/shard_map/reshape | solution.py:747
  4.0 107.2 %shard_map.82 = bf16[1,32,4096]{2,1,0:T(8,128)(2,1)} custom-call(bf16[4,2,32,1024]{3,2,1,0:T(8,128)(2,1)} %bitcast.5, bf16[1024,4096]{1,0:T(8,128)(2,1)} %wo.1, bf16[1,4096]{1,0:T(2,128)(2,1)} %reshape.21.gain, bf16[4096,512]{1,0:T(8,128)(2,1)} %wq.1, bf16[2,4096,128]{2,1,0:T(8,128)(2,1)} %wkv.1, bf16[2,1024,1024]{2,1,0:T(8,128)(2,1)} %bitcast.4, ...), custom_call_target="tpu_custom_call" | custom-call | tf_op jit(solution)/shard_map/pallas_call | solution.py:693
  111.2 1.7 %copy.12 = bf16[1,32,4096]{2,1,0:T(8,128)(2,1)} copy(bf16[1,32,4096]{2,1,0:T(8,128)(2,1)} %shard_map.82) | data formatting | bytes 524288
  (2 shorter events, 0.0 us)

commit v3 on v2

--- a/solution.py
+++ b/solution.py
@@ -122,7 +122,7 @@
 
 
 MESH = pl.DeviceIdType.MESH
-CHUNKS = 4
+CHUNKS = 2
 BF = jnp.bfloat16
 F32 = jnp.float32
 
@@ -136,8 +136,8 @@
     wkv,
     cache,
     lengths,
-    cosf,
-    sinf,
+    starts,
+    freqs,
     out,
     hid_v,
     wo_v,
@@ -161,6 +161,7 @@
     o_merged,
     fin,
     f_recv,
+    rope_v,
     in_sem,
     wo_sem,
     kvl_sem,
@@ -429,7 +430,7 @@
         x = x_all[k].reshape(span, cw).astype(F32)
         ssq[...] += jnp.sum(x * x, axis=-1, keepdims=True)
         cols = pl.ds(pl.multiple_of(k * cw, cw), cw)
-        xg = (x * gain[:, cols].astype(F32)).astype(BF)
+        xg = (x * gain[cols].astype(F32).reshape(1, cw)).astype(BF)
         acc[...] += jnp.dot(xg, w_v[cols, :], preferred_element_type=F32)
 
     def staggered(step, carry):
@@ -456,11 +457,17 @@
 
         return carry
 
+    angle = (starts[0] + lax.broadcasted_iota(jnp.int32, (span, HD), 0)).astype(F32) * freqs[...]
+    rope_v[0] = jnp.cos(angle)
+    sines = jnp.sin(angle)
+    first = lax.broadcasted_iota(jnp.int32, (span, HD), 1) < HD // 2
+    rope_v[1] = jnp.where(first, -sines, sines)
+
     lax.fori_loop(0, CHUNKS + 3, staggered, 0)
 
     inverse = lax.rsqrt(ssq[...] * (1.0 / width) + EPS)
-    cosine = cosf[...]
-    sine = sinf[...]
+    cosine = rope_v[0]
+    sine = rope_v[1]
 
     def rope(value):
         return value * cosine + pltpu.roll(value, HD // 2, 1) * sine
@@ -679,12 +686,7 @@
     wl = kv_cache.shape[2]
     half = HD // 2
     freq = THETA ** (-jnp.arange(half, dtype=F32) * 2.0 / HD)
-    positions = span_start[0] + jnp.arange(span, dtype=jnp.int32)
-    angle = positions.astype(F32)[:, None] * freq
-    cosine = jnp.cos(angle)
-    sine = jnp.sin(angle)
-    cosf = jnp.concatenate([cosine, cosine], axis=-1)
-    sinf = jnp.concatenate([-sine, sine], axis=-1)
+    freqs = jnp.concatenate([freq, freq])[None, :]
     any_spec = pl.BlockSpec(memory_space=pl.ANY)
     vm_spec = pl.BlockSpec(memory_space=pltpu.VMEM)
     sm_spec = pl.BlockSpec(memory_space=pltpu.SMEM)
@@ -693,7 +695,7 @@
     return pl.pallas_call(
         functools.partial(fused_kernel, Z),
         out_shape=jax.ShapeDtypeStruct((1, rows, 2 * Z * ql), BF),
-        in_specs=[any_spec, any_spec, vm_spec, any_spec, any_spec, any_spec, sm_spec, vm_spec, vm_spec],
+        in_specs=[any_spec, any_spec, vm_spec, any_spec, any_spec, any_spec, sm_spec, sm_spec, vm_spec],
         out_specs=vm_spec,
         scratch_shapes=[
             V((2, Z, rows, dl), BF),
@@ -718,6 +720,7 @@
             V((Z, 2, 2 * rows, ql + HD), BF),
             V((Z, 2 * rows, ql), BF),
             V((Z, rows, ql), BF),
+            V((2, span, HD), F32),
             dma((5,)),
             dma((CHUNKS,)),
             dma((2, Z)),
@@ -744,13 +747,13 @@
     )(
         gen_hidden.reshape(Z, 2, rows, dl),
         out_proj,
-        norm_gain.reshape(1, width),
+        norm_gain,
         q_weight,
         kv_weight,
         kv_cache.reshape(2, wl, KVH * HD),
         lengths,
-        cosf,
-        sinf,
+        span_start,
+        freqs,
     )
 
 

time: 113 us -> 109 us (0.965)
  Pallas kernels: 107 us -> 105 us
  local copies, waits for them, and re-layouts: 2.98 us -> 1.67 us
    pallas_call x1, Pallas kernels: 107 us -> 105 us  [fused(): pl.pallas_call(functools.partial(fused_kernel, Z), out_shape=jax.ShapeDty...]
    reshape x1 -> x0, local copies, waits for them, and re-layouts: 1.31 us -> none  [fused(): norm_gain.reshape(1, width)]
where the time goes in v3:
time: 109 us
  Pallas kernels  105 us (96%)
  local copies, waits for them, and re-layouts  1.67 us (2%)
  between operations  1.31 us (1%)
    pallas_call x1, Pallas kernels, fused(): pl.pallas_call(functools.partial(fused_kernel, Z), out_shape=jax.ShapeDty...  105 us

profile of v3, /device:TPU:0, one launch (start us, length us, event | category | flops | bytes accessed | tf_op | source)
XLA Modules:
  0.0 108.9 jit_solution(7264793422413973004)
XLA Ops:
  1.3 0.6 maximum_bitcast_fusion.freqs
  1.9 105.3 %shard_map.82 = bf16[1,32,4096]{2,1,0:T(8,128)(2,1)} custom-call(bf16[4,2,32,1024]{3,2,1,0:T(8,128)(2,1)} %bitcast.5, bf16[1024,4096]{1,0:T(8,128)(2,1)} %wo.1, bf16[4096]{0:T(1024)(128)(2,1)} %gain.1, bf16[4096,512]{1,0:T(8,128)(2,1)} %wq.1, bf16[2,4096,128]{2,1,0:T(8,128)(2,1)} %wkv.1, bf16[2,1024,1024]{2,1,0:T(8,128)(2,1)} %bitcast.4, ...), custom_call_target="tpu_custom_call" | custom-call | tf_op jit(solution)/shard_map/pallas_call | solution.py:695
  107.2 1.7 %copy.12 = bf16[1,32,4096]{2,1,0:T(8,128)(2,1)} copy(bf16[1,32,4096]{2,1,0:T(8,128)(2,1)} %shard_map.82) | data formatting | bytes 524288
  (1 shorter events, 0.0 us)

commit v4 on v3

--- a/solution.py
+++ b/solution.py
@@ -334,12 +334,12 @@
         pair_copy(k).wait_recv()
         both = own_part[k] + p_recv[k].astype(F32)
         rs_send[k] = both.astype(BF).reshape(Z, rows, cw)
+        @pl.when(jnp.logical_not(inner))
+        def _():
+            rs_copy(k, 3, far_out).start()
+            rs_copy(k, 2, far_in).start()
+
         rs_copy(k, 1, near).start()
-
-        @pl.when(jnp.logical_not(inner))
-        def _():
-            rs_copy(k, 2, far_in).start()
-            rs_copy(k, 3, far_out).start()
 
     def stage_a(k, carry):
         wo_copy(k).wait()
@@ -374,7 +374,7 @@
             kv_remote(i, j).start()
 
     def merge_rs(k):
-        for which, who in ((0, far_in), (1, far_out)):
+        for which, who in ((1, far_out), (0, far_in)):
             rs_copy(k, 2 + which, who).wait_recv()
             both = rs_send[k, who].astype(F32) + rs_recv[k, 2 + which].astype(F32)
             rs_merged[k, which] = both.astype(BF)
@@ -529,12 +529,12 @@
 
         stats = lax.fori_loop(0, heads, head, jnp.zeros((span, HD), F32))
         o_send[j, :, ql : ql + HD] = packed_stats(stats, span)
+        @pl.when(jnp.logical_not(inner))
+        def _():
+            o_copy(j, 3, far_out).start()
+            o_copy(j, 2, far_in).start()
+
         o_copy(j, 1, near).start()
-
-        @pl.when(jnp.logical_not(inner))
-        def _():
-            o_copy(j, 2, far_in).start()
-            o_copy(j, 3, far_out).start()
 
     def joined(parts):
         stats = []
@@ -554,7 +554,7 @@
         return mixes, best + jnp.log2(total)
 
     def merge_o(j):
-        for which, who in ((0, far_in), (1, far_out)):
+        for which, who in ((1, far_out), (0, far_in)):
             o_copy(j, 2 + which, who).wait_recv()
             mixes, lse = joined((o_send[j, chip_rows(who), :], o_recv[2 + which, j]))
             for h in range(heads):

time: 109 us -> 104 us (0.954)
  Pallas kernels: 105 us -> 100 us
    pallas_call x1, Pallas kernels: 105 us -> 100 us  [fused(): pl.pallas_call(functools.partial(fused_kernel, Z), out_shape=jax.ShapeDty...]
where the time goes in v4:
time: 104 us
  Pallas kernels  100 us (96%)
  local copies, waits for them, and re-layouts  1.67 us (2%)
  between operations  1.31 us (1%)
    pallas_call x1, Pallas kernels, fused(): pl.pallas_call(functools.partial(fused_kernel, Z), out_shape=jax.ShapeDty...  100 us

profile of v4, /device:TPU:0, one launch (start us, length us, event | category | flops | bytes accessed | tf_op | source)
XLA Modules:
  0.0 103.8 jit_solution(628250174684530463)
XLA Ops:
  1.3 0.6 maximum_bitcast_fusion.freqs
  1.9 100.2 %shard_map.82 = bf16[1,32,4096]{2,1,0:T(8,128)(2,1)} custom-call(bf16[4,2,32,1024]{3,2,1,0:T(8,128)(2,1)} %bitcast.5, bf16[1024,4096]{1,0:T(8,128)(2,1)} %wo.1, bf16[4096]{0:T(1024)(128)(2,1)} %gain.1, bf16[4096,512]{1,0:T(8,128)(2,1)} %wq.1, bf16[2,4096,128]{2,1,0:T(8,128)(2,1)} %wkv.1, bf16[2,1024,1024]{2,1,0:T(8,128)(2,1)} %bitcast.4, ...), custom_call_target="tpu_custom_call" | custom-call | tf_op jit(solution)/shard_map/pallas_call | solution.py:695
  102.1 1.7 %copy.12 = bf16[1,32,4096]{2,1,0:T(8,128)(2,1)} copy(bf16[1,32,4096]{2,1,0:T(8,128)(2,1)} %shard_map.82) | data formatting | bytes 524288
  (1 shorter events, 0.0 us)
